TPU v7x, 32 devices: a whole 2x2x4 slice. The times are simulated.
32 devices in a mesh: freq: 2 (over x), tile: 16 (over z, y, core).
Axes of the slice: x: 2, y: 2, z: 4, core: 2. Of those that a mesh axis runs over, the one named last changes fastest.
Arguments:
- data: float32 [4, 2048, 256], P('freq', 'tile'), parts along dimension 0, may hold values from -6 to 6
- x_init: float32 [4, 8192, 256], P('freq', 'tile'), parts along dimension 0, may hold values from -6 to 6
- ufac: bfloat16 [4, 2048, 256], P('freq', 'tile'), parts along dimension 0, may hold values from -0.1875 to 0.1875
- vfac: bfloat16 [4, 4, 16, 8192], P('freq', None, None, 'tile'), parts along dimension 0, may hold values from -0.25 to 0.25
Outputs:
- solution: float32 [4, 8192, 256], P('freq', 'tile'), parts along dimension 0
- residual: float32 [4, 2048, 256], P('freq', 'tile'), parts along dimension 0
There are 2 independent parts, one for each index of `freq`. A program takes and returns all parts, laid end to end along the dimension named above; each array names one. Nothing has to cross between parts.
All inputs are finite; a program needn't handle non-finite values.
Results may differ from a plain program's by a relative error of at most 0.0058.
Values may be sent and summed in bfloat16 or wider, within the bound.
No kernel may reach another device: no remote copies, remote signals or barrier semaphores. Data moves between devices by JAX's collectives and lax.ppermute only.
A program may use at most 64 MiB of HBM per device.

v0:
```python
import jax
import jax.numpy as jnp
from jax import lax
from jax.sharding import PartitionSpec as P

QV = 4
ITERS = 2
step_size = 0.4
threshold = 0.4


def complex_product(pattern, factors, vectors, conjugate):

    def single(factor_part, vector_part):
        return jnp.einsum(pattern, factor_part, vector_part, preferred_element_type=jnp.float32)

    if conjugate:
        real_part = single(factors[0], vectors[0]) + single(factors[1], vectors[1])
        imag_part = single(factors[0], vectors[1]) - single(factors[1], vectors[0])
    else:
        real_part = single(factors[0], vectors[0]) - single(factors[1], vectors[1])
        imag_part = single(factors[0], vectors[1]) + single(factors[1], vectors[0])
    return jnp.stack([real_part, imag_part])


def shrink(values):
    magnitude = jnp.sqrt(values[0] * values[0] + values[1] * values[1])
    shrink_factor = jnp.maximum(magnitude - threshold, 0.0) / jnp.maximum(magnitude, threshold)
    return values * shrink_factor


def body(data, x_init, ufac, vfac):
    tile_count = lax.axis_size("tile")
    tile_rows = vfac.shape[1]
    rank_width = vfac.shape[2]
    point_count = x_init.shape[2]
    estimate = x_init
    misfit = data
    for iteration in range(ITERS):
        xlow = estimate.astype(jnp.bfloat16)
        coeffs = complex_product("irk,kv->irv", vfac, xlow, True).astype(jnp.bfloat16)
        repeated = jnp.repeat(coeffs, QV, axis=1)
        received = lax.all_to_all(repeated, "tile", split_axis=1, concat_axis=1, tiled=True)
        flat_coeffs = received.reshape(2, tile_count * rank_width, point_count)
        predicted = complex_product("tk,kv->tv", ufac, flat_coeffs, False)
        misfit = data - predicted
        misfit_low = misfit.astype(jnp.bfloat16)
        partial_value = complex_product("tk,tv->kv", ufac, misfit_low, True).reshape(
            2, tile_count, rank_width, point_count
        )
        gathered = lax.all_to_all(partial_value, "tile", split_axis=1, concat_axis=1, tiled=True)
        summed = (
            gathered.reshape(2, tile_rows, QV, rank_width, point_count)
            .sum(axis=2)
            .astype(jnp.bfloat16)
        )
        gradient = complex_product("irk,irv->kv", vfac, summed, False)
        estimate = shrink(estimate + step_size * gradient)
    return (estimate, misfit)


def solution(mesh):
    in_specs = (
        P("freq", "tile", None),
        P("freq", "tile", None),
        P("freq", "tile", None),
        P("freq", None, None, "tile"),
    )
    out_specs = (P("freq", "tile", None), P("freq", "tile", None))
    return jax.shard_map(body, mesh=mesh, in_specs=in_specs, out_specs=out_specs, check_vma=False)
```

profile of v0, /device:TPU:0, one launch (start us, length us, event | category | flops | bytes accessed | tf_op | source)
XLA Modules:
  0.0 85.4 jit_solution(18116899990691036280)
XLA Ops:
  0.6 1.3 %convert_element_type.20 = bf16[2,512,256]{2,1,0:T(8,128)(2,1)S(1)} convert(f32[2,512,256]{2,1,0:T(8,128)} %param.5) | non-fusion elementwise | flops 262144 | bytes 1572864 | tf_op jit(solution)/shard_map/convert_element_type | solution.py:40
  2.7 0.7 broadcast_in_dim.8
  3.4 7.5 %all-to-all-start = ((bf16[2,16,16,256]{3,2,0,1:T(8,128)(2,1)}), bf16[2,16,16,256]{3,2,0,1:T(8,128)(2,1)S(1)}, u32[]{:S(2)}, u32[]{:S(2)}) async-start(bf16[2,16,16,256]{3,2,0,1:T(8,128)(2,1)} %bitcast.8), calls=%async_computation | async-start | bytes 524288 | tf_op jit(solution)/shard_map/all_to_all | solution.py:43
  11.1 9.9 %all-to-all-done = bf16[2,16,16,256]{3,2,0,1:T(8,128)(2,1)S(1)} async-done(((bf16[2,16,16,256]{3,2,0,1:T(8,128)(2,1)}), bf16[2,16,16,256]{3,2,0,1:T(8,128)(2,1)S(1)}, u32[]{:S(2)}, u32[]{:S(2)}) %all-to-all-start) | async-done | bytes 262176 | tf_op jit(solution)/shard_map/all_to_all | solution.py:43
  22.9 0.8 pad_maximum_fusion
  23.8 3.6 %all-to-all-start.1 = ((f32[2,16,16,256]{3,2,0,1:T(8,128)}), f32[2,16,16,256]{3,2,0,1:T(8,128)S(1)}, u32[]{:S(2)}, u32[]{:S(2)}) async-start(f32[2,16,16,256]{3,2,0,1:T(8,128)} %pad_maximum_fusion), calls=%async_computation.1 | async-start | bytes 1048576 | tf_op jit(solution)/shard_map/all_to_all | solution.py:51
  27.3 0.3 copy.35
  27.7 13.9 %all-to-all-done.1 = f32[2,16,16,256]{3,2,0,1:T(8,128)S(1)} async-done(((f32[2,16,16,256]{3,2,0,1:T(8,128)}), f32[2,16,16,256]{3,2,0,1:T(8,128)S(1)}, u32[]{:S(2)}, u32[]{:S(2)}) %all-to-all-start.1) | async-done | bytes 524320 | tf_op jit(solution)/shard_map/all_to_all | solution.py:51
  41.9 0.2 convolution_bitcast_fusion.4
  42.1 0.3 fusion.1
  42.9 0.3 divide_bitcast_fusion.1
  43.1 0.3 multiply_convert_fusion
  44.3 13.9 %all_to_all.20 = bf16[2,16,16,256]{3,2,0,1:T(8,128)(2,1)S(1)} all-to-all(bf16[2,16,16,256]{3,2,0,1:T(8,128)(2,1)S(1)} %bitcast.250), channel_id=1, replica_groups=mesh['freq'=2,'tile'=16] {'tile'}, dimensions={1} | all-to-all | bytes 524288 | tf_op jit(solution)/shard_map/all_to_all | solution.py:43
  59.2 0.7 fusion.103
  60.8 0.8 pad_maximum_fusion.1
  61.7 3.7 %all-to-all-start.3 = ((f32[2,16,16,256]{3,2,0,1:T(8,128)}), f32[2,16,16,256]{3,2,0,1:T(8,128)S(1)}, u32[]{:S(2)}, u32[]{:S(2)}) async-start(f32[2,16,16,256]{3,2,0,1:T(8,128)} %pad_maximum_fusion.1), calls=%async_computation.3 | async-start | bytes 1048576 | tf_op jit(solution)/shard_map/all_to_all | solution.py:51
  65.4 0.8 copy.46
  66.2 13.4 %all-to-all-done.3 = f32[2,16,16,256]{3,2,0,1:T(8,128)S(1)} async-done(((f32[2,16,16,256]{3,2,0,1:T(8,128)}), f32[2,16,16,256]{3,2,0,1:T(8,128)S(1)}, u32[]{:S(2)}, u32[]{:S(2)}) %all-to-all-start.3) | async-done | bytes 524320 | tf_op jit(solution)/shard_map/all_to_all | solution.py:51
  79.9 0.2 convolution_bitcast_fusion
  80.2 0.3 fusion.5
  80.7 0.4 fusion.21
  81.1 0.3 divide_bitcast_fusion
  81.4 1.5 %broadcast_multiply_fusion = f32[2,512,256]{1,2,0:T(8,128)} fusion(f32[512,256]{0,1:T(8,128)S(1)} %divide_bitcast_fusion, f32[1,512,256]{1,2,0:T(8,128)S(1)} %fusion.7, f32[1,512,256]{1,2,0:T(8,128)S(1)} %fusion.5, f32[512,256]{0,1:T(8,128)S(1)} %divide_bitcast_fusion.1, f32[2,512,256]{1,2,0:T(8,128)S(1)} %copy.35, f32[1,512,256]{1,2,0:T(8,128)S(1)} %fusion.3, ...), kind=kLoop, calls=%fused_computation.57 | loop fusion | flops 2097152 | bytes 5242880 | tf_op jit(solution)/shard_map/mul | solution.py:29
  82.9 2.5 %copy.45 = f32[2,512,256]{2,1,0:T(8,128)} copy(f32[2,512,256]{1,2,0:T(8,128)} %broadcast_multiply_fusion) | data formatting | bytes 2097152
  (52 shorter events, 6.6 us)
Async XLA Ops:
  0.6 1.3 %copy-start.2 = (bf16[2,4,16,512]{3,2,1,0:T(8,128)(2,1)S(1)}, bf16[2,4,16,512]{3,2,1,0:T(8,128)(2,1)}, u32[]{:S(2)}) copy-start(bf16[2,4,16,512]{3,2,1,0:T(8,128)(2,1)} %param.7) | copy-start | bytes 393220
  3.4 7.6 %copy-start.5 = (f32[2,128,256]{2,1,0:T(8,128)S(1)}, f32[2,128,256]{2,1,0:T(8,128)}, u32[]{:S(2)}) copy-start(f32[2,128,256]{2,1,0:T(8,128)} %param.4) | copy-start | bytes 786436
  3.4 17.6 %all-to-all-start = ((bf16[2,16,16,256]{3,2,0,1:T(8,128)(2,1)}), bf16[2,16,16,256]{3,2,0,1:T(8,128)(2,1)S(1)}, u32[]{:S(2)}, u32[]{:S(2)}) async-start(bf16[2,16,16,256]{3,2,0,1:T(8,128)(2,1)} %bitcast.8), calls=%async_computation | async-start | bytes 524288 | tf_op jit(solution)/shard_map/all_to_all | solution.py:43
  11.1 9.9 %copy-start = (bf16[2,128,256]{2,1,0:T(8,128)(2,1)S(1)}, bf16[2,128,256]{2,1,0:T(8,128)(2,1)}, u32[]{:S(2)}) copy-start(bf16[2,128,256]{2,1,0:T(8,128)(2,1)} %param.6) | copy-start | bytes 393220
  22.9 4.4 %copy-start.1 = (f32[2,512,256]{2,1,0:T(8,128)S(1)}, f32[2,512,256]{2,1,0:T(8,128)}, u32[]{:S(2)}) copy-start(f32[2,512,256]{2,1,0:T(8,128)} %param.5) | copy-start | bytes 3145732
  23.8 17.8 %all-to-all-start.1 = ((f32[2,16,16,256]{3,2,0,1:T(8,128)}), f32[2,16,16,256]{3,2,0,1:T(8,128)S(1)}, u32[]{:S(2)}, u32[]{:S(2)}) async-start(f32[2,16,16,256]{3,2,0,1:T(8,128)} %pad_maximum_fusion), calls=%async_computation.1 | async-start | bytes 1048576 | tf_op jit(solution)/shard_map/all_to_all | solution.py:51
  61.7 3.7 %copy-start.4 = (f32[2,128,256]{1,2,0:T(8,128)S(1)}, f32[2,128,256]{1,2,0:T(8,128)}, u32[]{:S(2)}) copy-start(f32[2,128,256]{1,2,0:T(8,128)} %get-tuple-element.9) | copy-start | bytes 786436
  61.7 17.9 %all-to-all-start.3 = ((f32[2,16,16,256]{3,2,0,1:T(8,128)}), f32[2,16,16,256]{3,2,0,1:T(8,128)S(1)}, u32[]{:S(2)}, u32[]{:S(2)}) async-start(f32[2,16,16,256]{3,2,0,1:T(8,128)} %pad_maximum_fusion.1), calls=%async_computation.3 | async-start | bytes 1048576 | tf_op jit(solution)/shard_map/all_to_all | solution.py:51
  66.2 13.4 %copy-start.3 = (bf16[2,4,16,512]{3,2,1,0:T(8,128)(2,1)S(1)}, bf16[2,4,16,512]{3,2,1,0:T(8,128)(2,1)}, u32[]{:S(2)}) copy-start(bf16[2,4,16,512]{3,2,1,0:T(8,128)(2,1)} %param.7) | copy-start | bytes 393220
where the time goes:
time: 85.9 us; the launch traced here: 85.4 us
  waiting for transfers between devices  37.1 us (43%)
  starting transfers between devices  14.8 us (17%)
  blocking collectives  13.9 us (16%)
  matrix products  7.03 us (8%)
  other arithmetic  6.81 us (8%)
  local copies, waits for them, and re-layouts  4.65 us (5%)
  between operations  1.04 us (1%)
    all_to_all x2, waiting for transfers between devices, body(): lax.all_to_all(partial_value, 'tile', split_axis=1, concat_axis=1, tiled=...  27.3 us
    all_to_all x1, blocking collectives, body(): lax.all_to_all(repeated, 'tile', split_axis=1, concat_axis=1, tiled=True)  13.9 us
    all_to_all x1, waiting for transfers between devices, body(): lax.all_to_all(repeated, 'tile', split_axis=1, concat_axis=1, tiled=True)  9.86 us
    all_to_all x1, starting transfers between devices, body(): lax.all_to_all(repeated, 'tile', split_axis=1, concat_axis=1, tiled=True)  7.55 us
    all_to_all x2, starting transfers between devices, body(): lax.all_to_all(partial_value, 'tile', split_axis=1, concat_axis=1, tiled=...  7.28 us
    dot_general x32, matrix products, single(): jnp.einsum(pattern, factor_part, vector_part, preferred_element_type=jnp....  7.03 us
    unnamed x16, local copies, waits for them, and re-layouts  3.85 us
    mul x3, other arithmetic, shrink(): return values * shrink_factor  1.99 us
  transfers between devices with their start and end apart: 3, of which 3 were waited for; matrix products, arithmetic and copies ran while one was open for 2% of the time, Pallas kernels for 0%

commit v1 on v0

--- a/solution.py
+++ b/solution.py
@@ -48,7 +48,9 @@
         partial_value = complex_product("tk,tv->kv", ufac, misfit_low, True).reshape(
             2, tile_count, rank_width, point_count
         )
-        gathered = lax.all_to_all(partial_value, "tile", split_axis=1, concat_axis=1, tiled=True)
+        pieces = jnp.split(partial_value, lax.axis_size("tile"), axis=1)
+        got = lax.all_to_all(jnp.stack(pieces), "tile", 0, 0)
+        gathered = jnp.concatenate(got, axis=1)
         summed = (
             gathered.reshape(2, tile_rows, QV, rank_width, point_count)
             .sum(axis=2)

time: 85.9 us -> 104 us (1.21)
  other arithmetic: 6.81 us -> 24.9 us
    unnamed x0 -> x30, other arithmetic: none -> 18.5 us
    another operation x4 -> x2, other arithmetic: 1.68 us -> 0.02 us  [complex_product(): return jnp.stack([real_part, imag_part])]
    another operation x0 -> x2, other arithmetic: none -> 1.23 us  [body(): got = lax.all_to_all(jnp.stack(pieces), 'tile', 0, 0)]
    unnamed x16 -> x12, local copies, waits for them, and re-layouts: 3.85 us -> 4.79 us
where the time goes in v1:
time: 104 us; the launch traced here: 103 us
  waiting for transfers between devices  36.2 us (35%)
  other arithmetic  24.9 us (24%)
  starting transfers between devices  14.7 us (14%)
  blocking collectives  13.9 us (13%)
  matrix products  7.01 us (7%)
  local copies, waits for them, and re-layouts  5.58 us (5%)
  between operations  1.04 us (1%)
    all_to_all x2, waiting for transfers between devices, body(): got = lax.all_to_all(jnp.stack(pieces), 'tile', 0, 0)  26.3 us
    unnamed x30, other arithmetic  18.5 us
    all_to_all x1, blocking collectives, body(): lax.all_to_all(repeated, 'tile', split_axis=1, concat_axis=1, tiled=True)  13.9 us
    all_to_all x1, waiting for transfers between devices, body(): lax.all_to_all(repeated, 'tile', split_axis=1, concat_axis=1, tiled=True)  9.86 us
    all_to_all x1, starting transfers between devices, body(): lax.all_to_all(repeated, 'tile', split_axis=1, concat_axis=1, tiled=True)  7.55 us
    all_to_all x2, starting transfers between devices, body(): got = lax.all_to_all(jnp.stack(pieces), 'tile', 0, 0)  7.15 us
    dot_general x32, matrix products, single(): jnp.einsum(pattern, factor_part, vector_part, preferred_element_type=jnp....  7.01 us
    unnamed x12, local copies, waits for them, and re-layouts  4.79 us
  transfers between devices with their start and end apart: 3, of which 3 were waited for; matrix products, arithmetic and copies ran while one was open for 2% of the time, Pallas kernels for 0%

profile of v1, /device:TPU:0, one launch (start us, length us, event | category | flops | bytes accessed | tf_op | source)
XLA Modules:
  0.0 103.3 jit_solution(4358416414586980024)
XLA Ops:
  0.6 1.3 %convert_element_type.20 = bf16[2,512,256]{2,1,0:T(8,128)(2,1)S(1)} convert(f32[2,512,256]{2,1,0:T(8,128)} %param.5) | non-fusion elementwise | flops 262144 | bytes 1572864 | tf_op jit(solution)/shard_map/convert_element_type | solution.py:40
  2.7 0.7 broadcast_in_dim.8
  3.4 7.5 %all-to-all-start = ((bf16[2,16,16,256]{3,2,0,1:T(8,128)(2,1)}), bf16[2,16,16,256]{3,2,0,1:T(8,128)(2,1)S(1)}, u32[]{:S(2)}, u32[]{:S(2)}) async-start(bf16[2,16,16,256]{3,2,0,1:T(8,128)(2,1)} %bitcast.8), calls=%async_computation | async-start | bytes 524288 | tf_op jit(solution)/shard_map/all_to_all | solution.py:43
  11.1 9.9 %all-to-all-done = bf16[2,16,16,256]{3,2,0,1:T(8,128)(2,1)S(1)} async-done(((bf16[2,16,16,256]{3,2,0,1:T(8,128)(2,1)}), bf16[2,16,16,256]{3,2,0,1:T(8,128)(2,1)S(1)}, u32[]{:S(2)}, u32[]{:S(2)}) %all-to-all-start) | async-done | bytes 262176 | tf_op jit(solution)/shard_map/all_to_all | solution.py:43
  22.9 0.6 constant_dynamic-update-slice_fusion.15
  23.5 0.6 constant_dynamic-update-slice_fusion.14
  24.1 0.6 constant_dynamic-update-slice_fusion.13
  24.8 0.6 constant_dynamic-update-slice_fusion.12
  25.4 0.6 constant_dynamic-update-slice_fusion.11
  26.0 0.6 constant_dynamic-update-slice_fusion.10
  26.6 0.6 constant_dynamic-update-slice_fusion.9
  27.2 0.6 constant_dynamic-update-slice_fusion.8
  29.1 0.6 constant_dynamic-update-slice_fusion.5
  32.8 3.6 %all-to-all-start.1 = ((f32[16,2,1,16,256]{4,3,1,2,0:T(8,128)}), f32[16,2,1,16,256]{4,3,1,2,0:T(8,128)S(1)}, u32[]{:S(2)}, u32[]{:S(2)}) async-start(f32[16,2,1,16,256]{4,3,1,2,0:T(8,128)} %constant_dynamic-update-slice_fusion), calls=%async_computation.1 | async-start | bytes 1048576 | tf_op jit(solution)/shard_map/all_to_all | solution.py:52
  36.7 13.9 %all-to-all-done.1 = f32[16,2,1,16,256]{4,3,1,2,0:T(8,128)S(1)} async-done(((f32[16,2,1,16,256]{4,3,1,2,0:T(8,128)}), f32[16,2,1,16,256]{4,3,1,2,0:T(8,128)S(1)}, u32[]{:S(2)}, u32[]{:S(2)}) %all-to-all-start.1) | async-done | bytes 524320 | tf_op jit(solution)/shard_map/all_to_all | solution.py:52
  53.4 13.9 %all_to_all.20 = bf16[2,16,16,256]{3,2,0,1:T(8,128)(2,1)S(1)} all-to-all(bf16[2,16,16,256]{3,2,0,1:T(8,128)(2,1)S(1)} %bitcast.438), channel_id=1, replica_groups=mesh['freq'=2,'tile'=16] {'tile'}, dimensions={1} | all-to-all | bytes 524288 | tf_op jit(solution)/shard_map/all_to_all | solution.py:43
  68.2 0.7 fusion.135
  69.9 0.6 constant_dynamic-update-slice_fusion.31
  73.6 0.6 constant_dynamic-update-slice_fusion.25
  79.7 3.6 %all-to-all-start.3 = ((f32[16,2,1,16,256]{4,3,1,2,0:T(8,128)}), f32[16,2,1,16,256]{4,3,1,2,0:T(8,128)S(1)}, u32[]{:S(2)}, u32[]{:S(2)}) async-start(f32[16,2,1,16,256]{4,3,1,2,0:T(8,128)} %constant_dynamic-update-slice_fusion.16), calls=%async_computation.3 | async-start | bytes 1048576 | tf_op jit(solution)/shard_map/all_to_all | solution.py:52
  83.3 1.8 %copy.87 = f32[2,128,256]{2,1,0:T(8,128)} copy(f32[2,128,256]{1,2,0:T(8,128)} %get-tuple-element.7) | data formatting | bytes 524288
  85.1 12.4 %all-to-all-done.3 = f32[16,2,1,16,256]{4,3,1,2,0:T(8,128)S(1)} async-done(((f32[16,2,1,16,256]{4,3,1,2,0:T(8,128)}), f32[16,2,1,16,256]{4,3,1,2,0:T(8,128)S(1)}, u32[]{:S(2)}, u32[]{:S(2)}) %all-to-all-start.3) | async-done | bytes 524320 | tf_op jit(solution)/shard_map/all_to_all | solution.py:52
  99.3 1.5 %broadcast_multiply_fusion = f32[2,512,256]{1,2,0:T(8,128)} fusion(f32[512,256]{0,1:T(8,128)S(1)} %divide_bitcast_fusion, f32[1,512,256]{1,2,0:T(8,128)S(1)} %fusion.7, f32[1,512,256]{1,2,0:T(8,128)S(1)} %fusion.5, f32[512,256]{0,1:T(8,128)S(1)} %divide_bitcast_fusion.1, f32[2,512,256]{1,2,0:T(8,128)S(1)} %copy.63, f32[1,512,256]{1,2,0:T(8,128)S(1)} %fusion.3, ...), kind=kLoop, calls=%fused_computation.113 | loop fusion | flops 2097152 | bytes 5242880 | tf_op jit(solution)/shard_map/mul | solution.py:29
  100.8 2.5 %copy.86 = f32[2,512,256]{2,1,0:T(8,128)} copy(f32[2,512,256]{1,2,0:T(8,128)} %broadcast_multiply_fusion) | data formatting | bytes 2097152
  (78 shorter events, 22.1 us)
Async XLA Ops:
  0.6 1.3 %copy-start.2 = (bf16[2,4,16,512]{3,2,1,0:T(8,128)(2,1)S(1)}, bf16[2,4,16,512]{3,2,1,0:T(8,128)(2,1)}, u32[]{:S(2)}) copy-start(bf16[2,4,16,512]{3,2,1,0:T(8,128)(2,1)} %param.7) | copy-start | bytes 393220
  3.4 7.6 %copy-start.3 = (f32[2,128,256]{2,1,0:T(8,128)S(1)}, f32[2,128,256]{2,1,0:T(8,128)}, u32[]{:S(2)}) copy-start(f32[2,128,256]{2,1,0:T(8,128)} %param.4) | copy-start | bytes 786436
  3.4 17.6 %all-to-all-start = ((bf16[2,16,16,256]{3,2,0,1:T(8,128)(2,1)}), bf16[2,16,16,256]{3,2,0,1:T(8,128)(2,1)S(1)}, u32[]{:S(2)}, u32[]{:S(2)}) async-start(bf16[2,16,16,256]{3,2,0,1:T(8,128)(2,1)} %bitcast.8), calls=%async_computation | async-start | bytes 524288 | tf_op jit(solution)/shard_map/all_to_all | solution.py:43
  11.1 9.9 %copy-start = (bf16[2,128,256]{2,1,0:T(8,128)(2,1)S(1)}, bf16[2,128,256]{2,1,0:T(8,128)(2,1)}, u32[]{:S(2)}) copy-start(bf16[2,128,256]{2,1,0:T(8,128)(2,1)} %param.6) | copy-start | bytes 393220
  31.6 4.8 %copy-start.1 = (f32[2,512,256]{2,1,0:T(8,128)S(1)}, f32[2,512,256]{2,1,0:T(8,128)}, u32[]{:S(2)}) copy-start(f32[2,512,256]{2,1,0:T(8,128)} %param.5) | copy-start | bytes 3145732
  32.8 17.8 %all-to-all-start.1 = ((f32[16,2,1,16,256]{4,3,1,2,0:T(8,128)}), f32[16,2,1,16,256]{4,3,1,2,0:T(8,128)S(1)}, u32[]{:S(2)}, u32[]{:S(2)}) async-start(f32[16,2,1,16,256]{4,3,1,2,0:T(8,128)} %constant_dynamic-update-slice_fusion), calls=%async_computation.1 | async-start | bytes 1048576 | tf_op jit(solution)/shard_map/all_to_all | solution.py:52
  79.7 17.8 %all-to-all-start.3 = ((f32[16,2,1,16,256]{4,3,1,2,0:T(8,128)}), f32[16,2,1,16,256]{4,3,1,2,0:T(8,128)S(1)}, u32[]{:S(2)}, u32[]{:S(2)}) async-start(f32[16,2,1,16,256]{4,3,1,2,0:T(8,128)} %constant_dynamic-update-slice_fusion.16), calls=%async_computation.3 | async-start | bytes 1048576 | tf_op jit(solution)/shard_map/all_to_all | solution.py:52
